TPU v7x, 256 devices: a whole 4x4x8 slice. The times are simulated.
256 devices in a mesh: group: 8 (over y, z_hi), tp: 32 (over x, z_lo, core).
Axes of the slice: x: 4, y: 4, z: 8 (z_hi: 2, z_lo: 4; z = z_hi * 4 + z_lo), core: 2. Of those that a mesh axis runs over, the one named last changes fastest.
Arguments:
- queries: bfloat16 [8, 8, 2, 8192], P('group', None, None, 'tp'), may hold values from -24 to 24
- new_keys: bfloat16 [8, 8, 2, 1024], P('group', None, None, 'tp'), may hold values from -16 to 16
- new_values: bfloat16 [8, 8, 2, 1024], P('group', None, None, 'tp'), may hold values from -24 to 24
- key_pages: bfloat16 [8, 2048, 16, 1024], P('group', 'tp'), may hold values from -16 to 16
- value_pages: bfloat16 [8, 2048, 16, 1024], P('group', 'tp'), may hold values from -24 to 24
- page_owner: int32 [8, 2048], P('group', 'tp'), may hold values from 0 to 8, as said below
- page_fill: int32 [8, 2048], P('group', 'tp'), may hold values from 0 to 16, as said below
- target_slot: int32 [8, 8], P('group'), may hold values from 0 to 8, as said below
- out_weight: bfloat16 [8192, 8192], P(None, 'tp'), may hold values from -0.0625 to 0.0625
Outputs:
- projected: bfloat16 [8, 8, 2, 8192], P('group', None, None, 'tp')
Inputs may be any that keep to these rules, and one draw needn't show every extreme that they name: `page_owner`: the owning request slot, or 8 for a free page. Of each pair of groups g and g XOR (4) one is loaded (no free pages) and the other light; group 0 is light, and so is group 8 - 1 when 8 > 2. One device holds at most 16 pages of moving requests, and some device of every loaded group holds exactly 16. `page_fill`: 1 to 16 for a used page, 0 for a free one. `target_slot`: 8 for a request that stays. Every group has exactly one moving request; their slots in the partner group are distinct and own no pages there.
All inputs are finite; a program needn't handle non-finite values.
Results may differ from a plain program's by a relative error of at most 0.0065.
Values may be sent and summed in bfloat16 or wider, within the bound.
A program may use at most 64 MiB of HBM per device.

v0:
```python
import math
import jax
import jax.numpy as jnp
from jax import lax
from jax.sharding import PartitionSpec as P

HEADS = 64
KVH = 8
HD = 128
PAGE = 16
MOVE = 1
neg_big = -1e30


def side_by_side(arrays, axis, dim, along):
    ends, at = ([], 0)
    for a in arrays[:-1]:
        at += a.shape[along]
        ends.append(at)
    both = jnp.concatenate(arrays, axis=along)
    return tuple(jnp.split(lax.all_gather(both, axis, axis=dim, tiled=True), ends, axis=along))


def swapped(value, axis, distance):
    return lax.ppermute(value, axis, [(i, i ^ 1 << distance) for i in range(lax.axis_size(axis))])


def copy_for_each(value, axis):
    peers = lax.axis_size(axis)
    return lax.all_to_all(
        jnp.broadcast_to(value[None], (peers, *value.shape)), axis, 0, 0, tiled=True
    )


def taken_together(value, axis):
    return copy_for_each(value, axis).max(axis=0)


def split_up(value, dim, peers):
    before, after = (value.shape[:dim], value.shape[dim + 1 :])
    return jnp.moveaxis(value.reshape(*before, peers, -1, *after), dim, 0)


def summed_on_arrival(value, axis, dim):
    blocks = split_up(value, dim, lax.axis_size(axis))
    arrived = lax.all_to_all(blocks, axis, split_axis=0, concat_axis=0, tiled=True)
    return arrived.sum(axis=0)


def in_one_piece(arrays, axis, dim, along):
    columns = [a.reshape(*a.shape[:along], -1) for a in arrays]
    both = jnp.concatenate(columns, axis=along)
    out, at, finished = (summed_on_arrival(both, axis, dim), 0, [])
    for a, column in zip(arrays, columns):
        share = out[..., at : at + column.shape[along]]
        finished.append(share.reshape(*share.shape[:along], *a.shape[along:]))
        at += column.shape[along]
    return tuple(finished)


def laid_out(blocks, dim):
    blocks = jnp.moveaxis(blocks, 0, dim)
    shape = blocks.shape
    return blocks.reshape(*shape[:dim], shape[dim] * shape[dim + 1], *shape[dim + 2 :])


def collect(value, axis, dim):
    return laid_out(copy_for_each(value, axis), dim)


def merge_states(first, second):
    largest = jnp.maximum(first[0], second[0])
    scale_first = jnp.exp(first[0] - largest)
    scale_second = jnp.exp(second[0] - largest)
    return (
        largest,
        first[1] * scale_first + second[1] * scale_second,
        first[2] * scale_first[..., None] + second[2] * scale_second[..., None],
    )


def page_states(query_rows, key_block, value_block, owner_rows, fill_counts, row_count):
    page_count = key_block.shape[0]
    step_count = query_rows.shape[1]
    group_size = HEADS // KVH
    scale_factor = 1.0 / math.sqrt(HD)
    clipped = jnp.clip(owner_rows, 0, row_count - 1)
    query_page = jnp.take(query_rows, clipped, axis=0).reshape(
        page_count, step_count, KVH, group_size, HD
    )
    key_page = key_block.reshape(page_count, PAGE, KVH, HD)
    value_page = value_block.reshape(page_count, PAGE, KVH, HD)
    scores = (
        jnp.einsum("psgjd,ptgd->psgjt", query_page, key_page, preferred_element_type=jnp.float32)
        * scale_factor
    )
    live_token = (owner_rows < row_count)[:, None] & (
        lax.broadcasted_iota(jnp.int32, (page_count, PAGE), 1) < fill_counts[:, None]
    )
    token_mask = live_token[:, None, None, None, :]
    scores = jnp.where(token_mask, scores, neg_big)
    page_top = jnp.max(scores, axis=4).reshape(page_count, step_count * HEADS)
    member = owner_rows[None, :] == lax.broadcasted_iota(jnp.int32, (row_count, page_count), 0)
    row_top = jnp.max(jnp.where(member[:, :, None], page_top[None], neg_big), axis=1)
    top_page = jnp.take(row_top, clipped, axis=0).reshape(
        page_count, step_count, KVH, group_size, 1
    )
    weights = jnp.where(token_mask, jnp.exp(scores - top_page), 0.0).astype(jnp.bfloat16)
    weighted = jnp.einsum(
        "psgjt,ptgd->psgjd", weights, value_page, preferred_element_type=jnp.float32
    ).reshape(page_count, step_count * HEADS * HD)
    weight_sum = jnp.sum(weights.astype(jnp.float32), axis=4).reshape(
        page_count, step_count * HEADS
    )
    onehot = member.astype(jnp.float32)
    row_sum = jnp.dot(onehot, weight_sum)
    row_acc = jnp.dot(onehot, weighted)
    return (
        row_top.reshape(row_count, step_count, HEADS),
        row_sum.reshape(row_count, step_count, HEADS),
        row_acc.reshape(row_count, step_count, HEADS, HD),
    )


def new_token_states(query_heads, key_rows, value_rows, head_kv):
    row_count = key_rows.shape[0]
    step_count = key_rows.shape[1]
    scale_factor = 1.0 / math.sqrt(HD)
    key_heads = jnp.take(key_rows.reshape(row_count, step_count, KVH, HD), head_kv, axis=2)
    value_heads = jnp.take(
        value_rows.reshape(row_count, step_count, KVH, HD), head_kv, axis=2
    ).astype(jnp.float32)
    scores = (
        jnp.einsum("rshd,ruhd->rshu", query_heads, key_heads, preferred_element_type=jnp.float32)
        * scale_factor
    )
    causal = (
        lax.broadcasted_iota(jnp.int32, (step_count, step_count), 1)
        <= lax.broadcasted_iota(jnp.int32, (step_count, step_count), 0)
    )[None, :, None, :]
    scores = jnp.where(causal, scores, neg_big)
    largest = jnp.max(scores, axis=3)
    weights = jnp.where(causal, jnp.exp(scores - largest[..., None]), 0.0)
    return (largest, jnp.sum(weights, axis=3), jnp.einsum("rshu,ruhd->rshd", weights, value_heads))


def per_device(
    queries,
    new_keys,
    new_values,
    key_pages,
    value_pages,
    page_owner,
    page_fill,
    target_slot,
    out_weight,
):
    row_count = queries.shape[1]
    step_count = queries.shape[2]
    partner_bit = lax.axis_size("group").bit_length() - 2
    query_rows, key_rows, value_rows = (
        lax.all_gather(queries[0], "tp", axis=2, tiled=True),
        *side_by_side((new_keys[0], new_values[0]), "tp", 2, 0),
    )
    owners = page_owner[0]
    fill_counts = page_fill[0]
    slot_targets = target_slot[0]
    clipped = jnp.clip(owners, 0, row_count - 1)
    page_target = jnp.take(slot_targets, clipped)
    occupied = owners < row_count
    moving = occupied & (page_target < row_count)
    partner_targets = swapped(slot_targets, "group", partner_bit)
    slot_ids = lax.broadcasted_iota(jnp.int32, (row_count,), 0)
    mover_ids = lax.broadcasted_iota(jnp.int32, (MOVE, row_count), 0)
    their_moving = partner_targets < row_count
    their_rank = jnp.cumsum(their_moving.astype(jnp.int32)) - 1
    their_pick = their_moving[None, :] & (their_rank[None, :] == mover_ids)
    pick_rows = jnp.sum(their_pick.astype(jnp.int32) * partner_targets[None, :], axis=1)
    pick_valid = jnp.any(their_pick, axis=1)
    send_pick = pick_valid[:, None] & (pick_rows[:, None] == slot_ids[None, :])
    sent_queries = jnp.einsum(
        "mr,rsd->msd",
        send_pick.astype(jnp.bfloat16),
        query_rows,
        preferred_element_type=jnp.float32,
    ).astype(jnp.bfloat16)
    arrived_queries = swapped(sent_queries, "group", partner_bit)
    own_moving = slot_targets < row_count
    own_rank = jnp.cumsum(own_moving.astype(jnp.int32)) - 1
    page_rank = jnp.take(own_rank, clipped)
    local_rows = jnp.where(
        occupied, jnp.where(moving, row_count + page_rank, owners), row_count + MOVE
    )
    joined = page_states(
        jnp.concatenate([query_rows, arrived_queries], axis=0),
        key_pages[0],
        value_pages[0],
        local_rows,
        fill_counts,
        row_count + MOVE,
    )
    own_part = tuple((member_array[:row_count] for member_array in joined))
    theirs = tuple((member_array[row_count:] for member_array in joined))
    returned = swapped((theirs[0], theirs[1], theirs[2]), "group", partner_bit)
    placement_table = send_pick.astype(jnp.float32)
    placed_any = jnp.any(send_pick, axis=0)
    placed_max = jnp.where(
        placed_any[:, None, None], jnp.einsum("mr,msh->rsh", placement_table, returned[0]), neg_big
    )
    placed_sum = jnp.einsum("mr,msh->rsh", placement_table, returned[1])
    placed_acc = jnp.einsum("mr,mshd->rshd", placement_table, returned[2])
    states = merge_states(own_part, (placed_max, placed_sum, placed_acc))
    head_kv_all = lax.broadcasted_iota(jnp.int32, (HEADS,), 0) // (HEADS // KVH)
    query_heads = query_rows.reshape(row_count, step_count, HEADS, HD)
    largest = taken_together(states[0], "tp")
    shrink = jnp.exp(states[0] - largest)
    share_sum, share_acc = in_one_piece(
        (states[1] * shrink, states[2] * shrink[..., None]), "tp", 2, 3
    )
    share_heads = share_sum.shape[2]
    first_head = lax.axis_index("tp") * share_heads
    share_largest = lax.dynamic_slice_in_dim(largest, first_head, share_heads, 2)
    share_query = lax.dynamic_slice_in_dim(query_heads, first_head, share_heads, 2)
    share_kv = lax.dynamic_slice_in_dim(head_kv_all, first_head, share_heads, 0)
    new_terms = new_token_states(share_query, key_rows, value_rows, share_kv)
    finished = merge_states((share_largest, share_sum, share_acc), new_terms)
    share_attention = (finished[2] / finished[1][..., None]).astype(jnp.bfloat16)
    attention = collect(share_attention, "tp", 2).reshape(row_count * step_count, HEADS * HD)
    projected = jnp.dot(attention, out_weight, preferred_element_type=jnp.float32).astype(
        jnp.bfloat16
    )
    return projected.reshape(1, row_count, step_count, out_weight.shape[1])


def solution(mesh):
    placed = (
        P("group", None, None, "tp"),
        P("group", None, None, "tp"),
        P("group", None, None, "tp"),
        P("group", "tp", None, None),
        P("group", "tp", None, None),
        P("group", "tp"),
        P("group", "tp"),
        P("group", None),
        P(None, "tp"),
    )
    return jax.shard_map(
        per_device,
        mesh=mesh,
        in_specs=placed,
        out_specs=P("group", None, None, "tp"),
        check_vma=False,
    )
```

profile of v0, /device:TPU:1, one launch (start us, length us, event | category | flops | bytes accessed | tf_op | source)
XLA Modules:
  0.0 218.9 jit_solution(16080722643461589940)
XLA Ops:
  0.0 3.7 %collective-permute-start = (s32[8]{0:T(128)}, s32[8]{0:T(128)S(1)}, u32[]{:S(2)}, u32[]{:S(2)}) collective-permute-start(s32[8]{0:T(128)} %bitcast.157), channel_id=1, source_target_pairs={{0,128},{32,160},{64,192},{96,224},{128,0},{160,32},{192,64},{224,... | collective-permute-start | bytes 104 | tf_op jit(solution)/shard_map/ppermute | solution.py:25
  3.7 1.6 fusion.48
  5.4 0.7 fusion.37
  6.0 0.2 reduce-window.18
  6.2 0.7 fusion.49
  6.9 10.6 %broadcast_compare_fusion = (pred[64]{0:T(512)(128)(4,1)S(1)}, s32[64]{0:T(128)S(1)}) fusion(s32[]{:T(128)} %bitcast.19, s32[]{:T(128)} %bitcast.18, s32[]{:T(128)} %bitcast.17, s32[]{:T(128)} %bitcast.16, s32[]{:T(128)} %bitcast.15, s32[]{:T(128)} %bitcast.14, s32[]{:T(128)} %bitcast.13, s32[]{:T(128)} %bitcast.12, s32[]{:T(128)} %bitcast.9, s32[]{:T(128)} %bitcast.8, ...), kind=kLoop, calls=%fused_computation.116 | loop fusion | flops 2368 | bytes 640 | tf_op jit(solution)/shard_map/lt | solution.py:97
  17.5 46.4 %all-gather = bf16[1,8,2,8192]{3,2,1,0:T(2,128)(2,1)S(1)} all-gather(bf16[1,8,2,256]{3,2,1,0:T(2,128)(2,1)} %param.13), channel_id=2, replica_groups=mesh['group'=8,'tp'=32] {'tp'}, dimensions={3}, use_global_device_ids=true | all-gather | bytes 270336 | tf_op jit(solution)/shard_map/all_gather | solution.py:162
  63.9 2.2 %copy.230 = bf16[128,8,8,128]{3,2,1,0:T(8,128)(2,1)S(1)} copy(bf16[128,8,8,128]{3,1,2,0:T(8,128)(2,1)} %bitcast.143) | data formatting | bytes 4194304
  66.2 1.5 bitcast_bitcast_fusion.1
  67.7 0.9 copy-done.1
  68.5 0.6 copy.231
  69.2 1.5 bitcast_bitcast_fusion
  71.0 40.1 %all_gather.7 = bf16[16,2,1024]{0,1,2:T(2,128)(2,1)S(1)} all-gather(bf16[16,2,32]{0,1,2:T(2,128)(2,1)S(1)} %pad_maximum_fusion.1), channel_id=1, replica_groups=mesh['group'=8,'tp'=32] {'tp'}, dimensions={2}, use_global_device_ids=true | all-gather | bytes 67584 | tf_op jit(solution)/shard_map/all_gather | solution.py:21
  111.1 0.2 reduce-window.19
  111.3 0.6 fusion.43
  111.9 0.7 select_reduce_fusion.1
  112.7 1.3 compare_and_fusion.2
  114.0 0.4 fusion.17
  114.5 0.1 collective-permute-start.1
  114.6 1.3 fusion.38
  115.9 2.9 %collective-permute-done.1 = bf16[1,2,8192]{2,1,0:T(2,128)(2,1)S(1)} collective-permute-done((bf16[1,2,8192]{2,1,0:T(2,128)(2,1)S(1)}, bf16[1,2,8192]{2,1,0:T(2,128)(2,1)S(1)}, u32[]{:S(2)}, u32[]{:S(2)}) %collective-permute-start.1) | collective-permute-done | bytes 32800 | tf_op jit(solution)/shard_map/ppermute | solution.py:25
  118.8 0.4 pad_maximum_fusion
  119.2 6.0 %gather_fusion = bf16[64,2,8192]{2,1,0:T(2,128)(2,1)S(1)} fusion(bf16[9,2,8192]{2,1,0:T(2,128)(2,1)S(1)} %pad_maximum_fusion, s32[1024]{0:T(1024)S(1)} %pad_clamp_fusion.1), kind=kCustom, calls=%fused_computation.2 | custom fusion | bytes 4194560 | tf_op jit(solution)/shard_map/jit(_take)/gather | solution.py:88
  125.3 2.9 %gather.19 = bf16[64,2,8,8,128]{4,3,2,1,0:T(8,128)(2,1)} reshape(bf16[64,2,8192]{2,1,0:T(2,128)(2,1)S(1)} %gather_fusion) | data formatting | bytes 4194304 | tf_op jit(solution)/shard_map/jit(_take)/gather | solution.py:88
  128.1 5.8 %bitcast_reduce_fusion = (f32[64,2,8,8]{3,1,2,0:T(2,128)S(1)}, f32[64,8,2,8,16]{4,3,2,1,0:T(8,128)}) fusion(pred[64,16]{1,0:T(8,128)(4,1)S(1)} %fusion.20, bf16[64,16,8,128,1]{3,2,1,0,4:T(8,128)(2,1)} %bitcast_bitcast_fusion.1, bf16[64,2,8,8,128]{4,3,2,1,0:T(8,128)(2,1)} %gather.19, pred[64]{0:T(512)(128)(4,1)S(1)} %get-tuple-element.18), kind=kOutput, calls=%fused_computation.8 | convolution fusion | flops 34988032 | bytes 4752448 | tf_op jit(solution)/shard_map/psgjd,ptgd->psgjt/dot_general | solution.py:94
  133.9 0.3 copy.178
  134.3 0.2 select_reduce_fusion
  134.5 0.6 gather_fusion.1
  135.2 0.3 collective-permute-start.2
  135.6 0.4 copy.181
  136.1 5.7 %convert_reduce_fusion = bf16[64,2,8,8]{3,1,2,0:T(2,128)(2,1)} fusion(f32[64,2,8,8]{3,1,2,0:T(2,128)S(1)} %copy.181, f32[64,8,2,8,16]{4,3,2,1,0:T(8,128)} %get-tuple-element.41, pred[64,16]{1,0:T(8,128)(4,1)S(1)} %fusion.20), kind=kLoop, calls=%fused_computation.12 | loop fusion | flops 909312 | bytes 574464 | tf_op jit(solution)/shard_map/reduce_sum | solution.py:112
  141.8 2.0 convolution_bitcast_fusion
  143.8 0.5 copy.188
  144.4 1.2 fusion
  145.8 0.2 copy.182
  146.1 0.8 reshape.380
  146.9 5.1 %all-to-all-start = ((f32[32,1,1024]{2,1,0:T(1,128)}), f32[32,1,1024]{2,1,0:T(1,128)S(1)}, u32[]{:S(2)}, u32[]{:S(2)}) async-start(f32[32,1,1024]{2,1,0:T(1,128)} %reshape.380), calls=%async_computation | async-start | bytes 262144 | tf_op jit(solution)/shard_map/all_to_all | solution.py:30
  152.4 2.9 %collective-permute-start.3 = (f32[1,2,64]{2,1,0:T(2,128)S(1)}, f32[1,2,64]{2,1,0:T(2,128)S(1)}, u32[]{:S(2)}, u32[]{:S(2)}) collective-permute-start(f32[1,2,64]{2,1,0:T(2,128)S(1)} %slice.49), channel_id=1, source_target_pairs={{0,128},{32,160},{64,192},{96,224},{128,0},{160,32},{192,64},{224,... | collective-permute-start | bytes 1544 | tf_op jit(solution)/shard_map/ppermute | solution.py:25
  155.3 5.5 %all-to-all-done = f32[32,1,1024]{2,1,0:T(1,128)S(1)} async-done(((f32[32,1,1024]{2,1,0:T(1,128)}), f32[32,1,1024]{2,1,0:T(1,128)S(1)}, u32[]{:S(2)}, u32[]{:S(2)}) %all-to-all-start) | async-done | bytes 131104 | tf_op jit(solution)/shard_map/all_to_all | solution.py:30
  160.8 0.5 broadcast.372
  161.3 0.9 reduce.12
  162.9 0.8 copy.192
  163.7 0.5 add_multiply_fusion
  164.2 0.3 maximum_bitcast_fusion
  164.6 1.1 copy.193
  165.7 5.3 %all-to-all-start.1 = ((f32[32,8,2,2,129]{4,1,3,2,0:T(8,128)}), f32[32,8,2,2,129]{4,1,3,2,0:T(8,128)S(1)}, u32[]{:S(2)}, u32[]{:S(2)}) async-start(f32[32,8,2,2,129]{4,1,3,2,0:T(8,128)} %copy.193), calls=%async_computation.1 | async-start | bytes 2097152 | tf_op jit(solution)/shard_map/all_to_all | solution.py:46
  171.0 0.9 fusion.47
  171.9 0.3 copy.199
  172.3 0.3 copy.204
  172.7 0.6 gather_fusion.2
  173.3 0.6 gather_fusion.3
  173.9 0.2 fusion.50
  174.1 0.1 copy.201
  174.4 24.4 %all-to-all-done.1 = f32[32,8,2,2,129]{4,1,3,2,0:T(8,128)S(1)} async-done(((f32[32,8,2,2,129]{4,1,3,2,0:T(8,128)}), f32[32,8,2,2,129]{4,1,3,2,0:T(8,128)S(1)}, u32[]{:S(2)}, u32[]{:S(2)}) %all-to-all-start.1) | async-done | bytes 528416 | tf_op jit(solution)/shard_map/all_to_all | solution.py:46
  199.0 0.2 copy.227
  199.3 0.1 copy.202
  199.5 0.1 copy.211
  199.7 0.2 fusion.15
  199.9 0.1 broadcast_in_dim.166
  200.1 14.9 %all_to_all.15 = bf16[32,8,2,2,128]{4,3,2,1,0:T(2,128)(2,1)S(1)} all-to-all(bf16[32,8,2,2,128]{4,3,2,1,0:T(2,128)(2,1)S(1)} %broadcast_in_dim.166), channel_id=1, replica_groups=mesh['group'=8,'tp'=32] {'tp'}, dimensions={0} | all-to-all | bytes 524288 | tf_op jit(solution)/shard_map/all_to_all | solution.py:30
  215.0 0.2 copy.213
  215.2 0.2 reshape_reshape.3
  215.4 2.8 %convolution_convert_fusion = bf16[16,256]{1,0:T(8,128)(2,1)S(1)} fusion(bf16[16,8192]{1,0:T(8,128)(2,1)S(1)} %reshape_reshape.3, bf16[8192,256]{1,0:T(8,128)(2,1)} %param.21), kind=kOutput, calls=%fused_computation.30 | convolution fusion | flops 67112960 | bytes 4464640 | tf_op jit(solution)/shard_map/dot_general | solution.py:229
  218.3 0.6 reshape.270
  (64 shorter events, 2.8 us)
Async XLA Ops:
  0.0 111.1 %collective-permute-start = (s32[8]{0:T(128)}, s32[8]{0:T(128)S(1)}, u32[]{:S(2)}, u32[]{:S(2)}) collective-permute-start(s32[8]{0:T(128)} %bitcast.157), channel_id=1, source_target_pairs={{0,128},{32,160},{64,192},{96,224},{128,0},{160,32},{192,64},{224,... | collective-permute-start | bytes 104 | tf_op jit(solution)/shard_map/ppermute | solution.py:25
  66.2 2.4 %copy-start.1 = (bf16[1,64,16,1024]{3,2,1,0:T(8,128)(2,1)S(1)}, bf16[1,64,16,1024]{3,2,1,0:T(8,128)(2,1)}, u32[]{:S(2)}) copy-start(bf16[1,64,16,1024]{3,2,1,0:T(8,128)(2,1)} %param.17) | copy-start | bytes 6291460
  69.2 1.5 copy-start.4
  69.2 1.6 copy-start.5
  69.2 41.8 %copy-start.6 = (s32[1,64]{1,0:T(1,128)S(1)}, s32[1,64]{1,0:T(1,128)}, u32[]{:S(2)}) copy-start(s32[1,64]{1,0:T(1,128)} %param.19) | copy-start | bytes 772
  114.5 4.4 %collective-permute-start.1 = (bf16[1,2,8192]{2,1,0:T(2,128)(2,1)S(1)}, bf16[1,2,8192]{2,1,0:T(2,128)(2,1)S(1)}, u32[]{:S(2)}, u32[]{:S(2)}) collective-permute-start(bf16[1,2,8192]{2,1,0:T(2,128)(2,1)S(1)} %copy.277), channel_id=1, source_target_pairs={{0,128},{32,160},{64,192},{96,224},{128,0},{160,32},{192,64},{224,... | collective-permute-start | bytes 98312 | tf_op jit(solution)/shard_map/ppermute | solution.py:25
  133.9 7.9 %copy-start.2 = (bf16[64,16,8,128,1]{3,2,1,0,4:T(8,128)(2,1)S(1)}, bf16[64,16,8,128,1]{3,2,1,0,4:T(8,128)(2,1)}, u32[]{:S(2)}) copy-start(bf16[64,16,8,128,1]{3,2,1,0,4:T(8,128)(2,1)} %bitcast_bitcast_fusion) | copy-start | bytes 6291460
  135.2 10.8 %collective-permute-start.2 = (f32[1,2,64]{2,1,0:T(2,128)S(1)}, f32[1,2,64]{2,1,0:T(2,128)S(1)}, u32[]{:S(2)}, u32[]{:S(2)}) collective-permute-start(f32[1,2,64]{2,1,0:T(2,128)S(1)} %slice.47), channel_id=1, source_target_pairs={{0,128},{32,160},{64,192},{96,224},{128,0},{160,32},{192,64},{224,... | collective-permute-start | bytes 1544 | tf_op jit(solution)/shard_map/ppermute | solution.py:25
  136.1 5.7 %copy-start = (f32[64,8,2,8,16]{4,3,2,1,0:T(8,128)S(1)}, f32[64,8,2,8,16]{4,3,2,1,0:T(8,128)}, u32[]{:S(2)}) copy-start(f32[64,8,2,8,16]{4,3,2,1,0:T(8,128)} %get-tuple-element.41) | copy-start | bytes 1572868
  144.3 1.4 copy-start.3
  146.9 13.9 %all-to-all-start = ((f32[32,1,1024]{2,1,0:T(1,128)}), f32[32,1,1024]{2,1,0:T(1,128)S(1)}, u32[]{:S(2)}, u32[]{:S(2)}) async-start(f32[32,1,1024]{2,1,0:T(1,128)} %reshape.380), calls=%async_computation | async-start | bytes 262144 | tf_op jit(solution)/shard_map/all_to_all | solution.py:30
  152.4 10.1 %collective-permute-start.3 = (f32[1,2,64]{2,1,0:T(2,128)S(1)}, f32[1,2,64]{2,1,0:T(2,128)S(1)}, u32[]{:S(2)}, u32[]{:S(2)}) collective-permute-start(f32[1,2,64]{2,1,0:T(2,128)S(1)} %slice.49), channel_id=1, source_target_pairs={{0,128},{32,160},{64,192},{96,224},{128,0},{160,32},{192,64},{224,... | collective-permute-start | bytes 1544 | tf_op jit(solution)/shard_map/ppermute | solution.py:25
  155.2 8.5 %collective-permute-start.4 = (f32[1,2,64,128]{3,2,1,0:T(8,128)S(1)}, f32[1,2,64,128]{3,2,1,0:T(8,128)S(1)}, u32[]{:S(2)}, u32[]{:S(2)}) collective-permute-start(f32[1,2,64,128]{3,2,1,0:T(8,128)S(1)} %bitcast.156), channel_id=1, source_target_pairs={{0,128},{32,160},{64,192},{96,224},{128,0},{160,32},{192,64},{224,... | collective-permute-start | bytes 196616 | tf_op jit(solution)/shard_map/ppermute | solution.py:25
  165.7 33.2 %all-to-all-start.1 = ((f32[32,8,2,2,129]{4,1,3,2,0:T(8,128)}), f32[32,8,2,2,129]{4,1,3,2,0:T(8,128)S(1)}, u32[]{:S(2)}, u32[]{:S(2)}) async-start(f32[32,8,2,2,129]{4,1,3,2,0:T(8,128)} %copy.193), calls=%async_computation.1 | async-start | bytes 2097152 | tf_op jit(solution)/shard_map/all_to_all | solution.py:46
where the time goes:
time: 220 us; the launch traced here: 219 us
  blocking collectives  101 us (46%)
  waiting for transfers between devices  32.8 us (15%)
  local copies, waits for them, and re-layouts  29.4 us (13%)
  other arithmetic  24.5 us (11%)
  starting transfers between devices  17.6 us (8%)
  matrix products  12.8 us (6%)
    all_gather x1, blocking collectives, per_device(): lax.all_gather(queries[0], 'tp', axis=2, tiled=True)  46.4 us
    all_gather x1, blocking collectives, side_by_side(): lax.all_gather(both, axis, axis=dim, tiled=True)  40.1 us
    all_to_all x1, waiting for transfers between devices, summed_on_arrival(): lax.all_to_all(blocks, axis, split_axis=0, concat_axis=0, tiled=True)  24.4 us
    all_to_all x1, blocking collectives, copy_for_each(): lax.all_to_all(jnp.broadcast_to(value[None], (peers, *value.shape)), axis...  14.9 us
    lt x1, other arithmetic, page_states(): owner_rows < row_count  10.6 us
    gather x2, local copies, waits for them, and re-layouts, page_states(): jnp.take(query_rows, clipped, axis=0)  8.91 us
    ppermute x5, starting transfers between devices, swapped(): lax.ppermute(value, axis, [(i, i ^ 1 << distance) for i in range(lax.axis...  7.21 us
    dot_general x1, matrix products, page_states(): jnp.einsum('psgjd,ptgd->psgjt', query_page, key_page, preferred_element_t...  5.79 us
  transfers between devices with their start and end apart: 7, of which 3 were waited for; matrix products, arithmetic and copies ran while one was open for 17% of the time, Pallas kernels for 0%

commit v1 on v0

--- a/solution.py
+++ b/solution.py
@@ -10,6 +10,13 @@
 PAGE = 16
 MOVE = 1
 neg_big = -1e30
+
+
+def exchange_gather(block, axis, dim):
+    n_dev = lax.axis_size(axis)
+    pieces = jnp.stack([block for _ in range(n_dev)])
+    pieces = lax.all_to_all(pieces, axis, split_axis=0, concat_axis=0)
+    return jnp.concatenate(pieces, axis=dim)
 
 
 def side_by_side(arrays, axis, dim, along):
@@ -159,7 +166,7 @@
     step_count = queries.shape[2]
     partner_bit = lax.axis_size("group").bit_length() - 2
     query_rows, key_rows, value_rows = (
-        lax.all_gather(queries[0], "tp", axis=2, tiled=True),
+        exchange_gather(queries[0], "tp", 2),
         *side_by_side((new_keys[0], new_values[0]), "tp", 2, 0),
     )
     owners = page_owner[0]

time: 220 us -> 193 us (0.88)
  blocking collectives: 101 us -> 60.5 us
  starting transfers between devices: 17.6 us -> 27.1 us
  local copies, waits for them, and re-layouts: 29.4 us -> 32.4 us
    all_gather x1 -> x0, blocking collectives: 46.4 us -> none  [per_device(): lax.all_gather(queries[0], 'tp', axis=2, tiled=True)]
    all_to_all x0 -> x1, starting transfers between devices: none -> 9.47 us  [exchange_gather(): pieces = lax.all_to_all(pieces, axis, split_axis=0, concat_axis=0)]
    all_gather x1, blocking collectives: 40.1 us -> 45.6 us  [side_by_side(): lax.all_gather(both, axis, axis=dim, tiled=True)]
    unnamed x21 -> x23, local copies, waits for them, and re-layouts: 4.86 us -> 4.86 us
  transfers between devices with their start and end apart: 7 -> 8, of which waited for: 3 -> 3; matrix products, arithmetic and copies ran while one was open for 17% -> 23% of each run, Pallas kernels for 0% -> 0%
where the time goes in v1:
time: 193 us; the launch traced here: 192 us
  blocking collectives  60.5 us (31%)
  waiting for transfers between devices  33.3 us (17%)
  local copies, waits for them, and re-layouts  32.4 us (17%)
  starting transfers between devices  27.1 us (14%)
  other arithmetic  24.3 us (13%)
  matrix products  13.8 us (7%)
    all_gather x1, blocking collectives, side_by_side(): lax.all_gather(both, axis, axis=dim, tiled=True)  45.6 us
    all_to_all x1, waiting for transfers between devices, summed_on_arrival(): lax.all_to_all(blocks, axis, split_axis=0, concat_axis=0, tiled=True)  25.1 us
    all_to_all x1, blocking collectives, copy_for_each(): lax.all_to_all(jnp.broadcast_to(value[None], (peers, *value.shape)), axis...  14.9 us
    lt x1, other arithmetic, page_states(): owner_rows < row_count  10.6 us
    all_to_all x1, starting transfers between devices, exchange_gather(): pieces = lax.all_to_all(pieces, axis, split_axis=0, concat_axis=0)  9.47 us
    gather x2, local copies, waits for them, and re-layouts, page_states(): jnp.take(query_rows, clipped, axis=0)  8.91 us
    ppermute x5, starting transfers between devices, swapped(): lax.ppermute(value, axis, [(i, i ^ 1 << distance) for i in range(lax.axis...  7.41 us
    dot_general x1, matrix products, page_states(): jnp.einsum('psgjd,ptgd->psgjt', query_page, key_page, preferred_element_t...  5.73 us
  transfers between devices with their start and end apart: 8, of which 3 were waited for; matrix products, arithmetic and copies ran while one was open for 23% of the time, Pallas kernels for 0%

profile of v1, /device:TPU:1, one launch (start us, length us, event | category | flops | bytes accessed | tf_op | source)
XLA Modules:
  0.0 191.9 jit_solution(15538681211634432526)
XLA Ops:
  0.0 3.7 %collective-permute-start = (s32[8]{0:T(128)}, s32[8]{0:T(128)S(1)}, u32[]{:S(2)}, u32[]{:S(2)}) collective-permute-start(s32[8]{0:T(128)} %bitcast.164), channel_id=1, source_target_pairs={{0,128},{32,160},{64,192},{96,224},{128,0},{160,32},{192,64},{224,... | collective-permute-start | bytes 104 | tf_op jit(solution)/shard_map/ppermute | solution.py:32
  3.7 1.5 stack.3
  5.3 9.5 %all-to-all-start = ((bf16[32,8,2,256]{3,2,1,0:T(2,128)(2,1)}), bf16[32,8,2,256]{3,2,1,0:T(2,128)(2,1)S(1)}, u32[]{:S(2)}, u32[]{:S(2)}) async-start(bf16[32,8,2,256]{3,2,1,0:T(2,128)(2,1)} %stack.3), calls=%async_computation | async-start | bytes 524288 | tf_op jit(solution)/shard_map/all_to_all | solution.py:18
  14.8 1.6 fusion.43
  16.4 0.7 fusion.35
  17.0 0.2 reduce-window.18
  17.2 0.7 fusion.44
  17.9 10.6 %broadcast_compare_fusion = (pred[64]{0:T(512)(128)(4,1)S(1)}, s32[64]{0:T(128)S(1)}) fusion(s32[]{:T(128)} %bitcast.19, s32[]{:T(128)} %bitcast.18, s32[]{:T(128)} %bitcast.17, s32[]{:T(128)} %bitcast.16, s32[]{:T(128)} %bitcast.15, s32[]{:T(128)} %bitcast.14, s32[]{:T(128)} %bitcast.13, s32[]{:T(128)} %bitcast.12, s32[]{:T(128)} %bitcast.9, s32[]{:T(128)} %bitcast.8, ...), kind=kLoop, calls=%fused_computation.114 | loop fusion | flops 2368 | bytes 640 | tf_op jit(solution)/shard_map/lt | solution.py:104
  28.6 2.2 %copy.256 = bf16[128,8,8,128]{3,2,1,0:T(8,128)(2,1)S(1)} copy(bf16[128,8,8,128]{3,1,2,0:T(8,128)(2,1)} %bitcast.150) | data formatting | bytes 4194304
  30.8 1.5 bitcast_bitcast_fusion.1
  32.3 0.9 copy-done.1
  33.1 0.6 copy.257
  33.8 1.5 bitcast_bitcast_fusion
  35.6 45.6 %all_gather.3 = bf16[16,2,1024]{0,1,2:T(2,128)(2,1)S(1)} all-gather(bf16[16,2,32]{0,1,2:T(2,128)(2,1)S(1)} %pad_maximum_fusion.1), channel_id=1, replica_groups=mesh['group'=8,'tp'=32] {'tp'}, dimensions={2}, use_global_device_ids=true | all-gather | bytes 67584 | tf_op jit(solution)/shard_map/all_gather | solution.py:28
  81.2 1.8 fusion.42
  83.0 0.2 reduce-window.19
  83.2 0.6 fusion.38
  83.9 0.6 select_reduce_fusion.1
  84.5 1.3 bitcast_convert_fusion.1
  86.0 1.5 fusion.30
  87.6 0.1 collective-permute-start.1
  87.7 1.3 compare_and_fusion.2
  89.0 0.3 copy.197
  89.3 2.7 %collective-permute-done.1 = bf16[1,2,8192]{2,1,0:T(2,128)(2,1)S(1)} collective-permute-done((bf16[1,2,8192]{2,1,0:T(2,128)(2,1)S(1)}, bf16[1,2,8192]{2,1,0:T(2,128)(2,1)S(1)}, u32[]{:S(2)}, u32[]{:S(2)}) %collective-permute-start.1) | collective-permute-done | bytes 32800 | tf_op jit(solution)/shard_map/ppermute | solution.py:32
  91.9 0.4 pad_maximum_fusion
  92.3 6.0 %gather_fusion = bf16[64,2,8192]{2,1,0:T(2,128)(2,1)S(1)} fusion(bf16[9,2,8192]{2,1,0:T(2,128)(2,1)S(1)} %pad_maximum_fusion, s32[1024]{0:T(1024)S(1)} %pad_clamp_fusion.1), kind=kCustom, calls=%fused_computation.2 | custom fusion | bytes 4194560 | tf_op jit(solution)/shard_map/jit(_take)/gather | solution.py:95
  98.4 2.9 %reshape.369 = bf16[64,2,8,8,128]{4,3,2,1,0:T(8,128)(2,1)} reshape(bf16[64,2,8192]{2,1,0:T(2,128)(2,1)S(1)} %gather_fusion) | data formatting | bytes 4194304 | tf_op jit(solution)/shard_map/jit(_take)/gather | solution.py:95
  101.2 5.7 %bitcast_reduce_fusion = (f32[64,2,8,8]{3,1,2,0:T(2,128)S(1)}, f32[64,8,2,8,16]{4,3,2,1,0:T(8,128)}) fusion(pred[64,16]{1,0:T(8,128)(4,1)S(1)} %fusion.17, bf16[64,16,8,128,1]{3,2,1,0,4:T(8,128)(2,1)} %bitcast_bitcast_fusion.1, bf16[64,2,8,8,128]{4,3,2,1,0:T(8,128)(2,1)} %reshape.369, pred[64]{0:T(512)(128)(4,1)S(1)} %get-tuple-element.18), kind=kOutput, calls=%fused_computation.8 | convolution fusion | flops 34988032 | bytes 4752448 | tf_op jit(solution)/shard_map/psgjd,ptgd->psgjt/dot_general | solution.py:101
  107.0 0.3 copy.201
  107.3 0.2 select_reduce_fusion
  107.5 0.6 gather_fusion.1
  108.2 0.6 collective-permute-start.2
  108.9 0.4 copy.204
  109.3 5.7 %convert_reduce_fusion = bf16[64,2,8,8]{3,1,2,0:T(2,128)(2,1)} fusion(f32[64,2,8,8]{3,1,2,0:T(2,128)S(1)} %copy.204, f32[64,8,2,8,16]{4,3,2,1,0:T(8,128)} %get-tuple-element.41, pred[64,16]{1,0:T(8,128)(4,1)S(1)} %fusion.17), kind=kLoop, calls=%fused_computation.12 | loop fusion | flops 909312 | bytes 574464 | tf_op jit(solution)/shard_map/reduce_sum | solution.py:119
  115.1 2.0 %convolution_bitcast_fusion = bf16[64,2,8,8,128]{4,3,1,2,0:T(8,128)(2,1)S(1)} fusion(bf16[64,16,8,128,1]{3,2,1,0,4:T(8,128)(2,1)S(1)} %copy-done.2, f32[64,8,2,8,16]{4,3,2,1,0:T(8,128)S(1)} %copy-done, f32[64,2,8,8]{3,1,2,0:T(2,128)S(1)} %copy.204, pred[64,16]{1,0:T(8,128)(4,1)S(1)} %fusion.17), kind=kOutput, calls=%fused_computation.14 | convolution fusion | flops 34209792 | bytes 4752384 | tf_op jit(solution)/shard_map/psgjt,ptgd->psgjd/dot_general | solution.py:116
  117.1 0.5 copy.211
  117.6 1.2 fusion
  119.0 0.2 copy.205
  119.3 0.8 reshape.382
  120.2 4.9 %all-to-all-start.1 = ((f32[32,1,1024]{2,1,0:T(1,128)}), f32[32,1,1024]{2,1,0:T(1,128)S(1)}, u32[]{:S(2)}, u32[]{:S(2)}) async-start(f32[32,1,1024]{2,1,0:T(1,128)} %reshape.382), calls=%async_computation.1 | async-start | bytes 262144 | tf_op jit(solution)/shard_map/all_to_all | solution.py:37
  125.4 2.9 %collective-permute-start.3 = (f32[1,2,64]{2,1,0:T(2,128)S(1)}, f32[1,2,64]{2,1,0:T(2,128)S(1)}, u32[]{:S(2)}, u32[]{:S(2)}) collective-permute-start(f32[1,2,64]{2,1,0:T(2,128)S(1)} %slice.49), channel_id=1, source_target_pairs={{0,128},{32,160},{64,192},{96,224},{128,0},{160,32},{192,64},{224,... | collective-permute-start | bytes 1544 | tf_op jit(solution)/shard_map/ppermute | solution.py:32
  128.4 5.5 %all-to-all-done.1 = f32[32,1,1024]{2,1,0:T(1,128)S(1)} async-done(((f32[32,1,1024]{2,1,0:T(1,128)}), f32[32,1,1024]{2,1,0:T(1,128)S(1)}, u32[]{:S(2)}, u32[]{:S(2)}) %all-to-all-start.1) | async-done | bytes 131104 | tf_op jit(solution)/shard_map/all_to_all | solution.py:37
  133.9 0.5 broadcast.381
  134.4 0.9 reduce.12
  136.0 0.8 copy.215
  136.8 0.5 add_multiply_fusion
  137.3 0.3 maximum_bitcast_fusion
  137.6 1.1 copy.216
  138.7 5.3 %all-to-all-start.2 = ((f32[32,8,2,2,129]{4,1,3,2,0:T(8,128)}), f32[32,8,2,2,129]{4,1,3,2,0:T(8,128)S(1)}, u32[]{:S(2)}, u32[]{:S(2)}) async-start(f32[32,8,2,2,129]{4,1,3,2,0:T(8,128)} %copy.216), calls=%async_computation.2 | async-start | bytes 2097152 | tf_op jit(solution)/shard_map/all_to_all | solution.py:53
  144.1 0.3 copy.222
  144.4 0.3 copy.229
  144.8 0.6 gather_fusion.2
  145.4 0.6 gather_fusion.3
  146.2 0.2 fusion.45
  146.7 25.1 %all-to-all-done.2 = f32[32,8,2,2,129]{4,1,3,2,0:T(8,128)S(1)} async-done(((f32[32,8,2,2,129]{4,1,3,2,0:T(8,128)}), f32[32,8,2,2,129]{4,1,3,2,0:T(8,128)S(1)}, u32[]{:S(2)}, u32[]{:S(2)}) %all-to-all-start.2) | async-done | bytes 528416 | tf_op jit(solution)/shard_map/all_to_all | solution.py:53
  172.0 0.2 copy.252
  172.3 0.1 copy.227
  172.7 0.2 fusion.15
  173.0 0.1 broadcast_in_dim.166
  173.1 14.9 %all_to_all.20 = bf16[32,8,2,2,128]{4,3,2,1,0:T(2,128)(2,1)S(1)} all-to-all(bf16[32,8,2,2,128]{4,3,2,1,0:T(2,128)(2,1)S(1)} %broadcast_in_dim.166), channel_id=1, replica_groups=mesh['group'=8,'tp'=32] {'tp'}, dimensions={0} | all-to-all | bytes 524288 | tf_op jit(solution)/shard_map/all_to_all | solution.py:37
  188.0 0.2 copy.238
  188.3 0.2 reshape_reshape.7
  188.5 2.8 %convolution_convert_fusion = bf16[16,256]{1,0:T(8,128)(2,1)S(1)} fusion(bf16[16,8192]{1,0:T(8,128)(2,1)S(1)} %reshape_reshape.7, bf16[8192,256]{1,0:T(8,128)(2,1)} %param.21), kind=kOutput, calls=%fused_computation.30 | convolution fusion | flops 67112960 | bytes 4464640 | tf_op jit(solution)/shard_map/dot_general | solution.py:236
  191.3 0.6 reshape.274
  (74 shorter events, 3.5 us)
Async XLA Ops:
  0.0 83.0 %collective-permute-start = (s32[8]{0:T(128)}, s32[8]{0:T(128)S(1)}, u32[]{:S(2)}, u32[]{:S(2)}) collective-permute-start(s32[8]{0:T(128)} %bitcast.164), channel_id=1, source_target_pairs={{0,128},{32,160},{64,192},{96,224},{128,0},{160,32},{192,64},{224,... | collective-permute-start | bytes 104 | tf_op jit(solution)/shard_map/ppermute | solution.py:32
  5.3 80.5 %all-to-all-start = ((bf16[32,8,2,256]{3,2,1,0:T(2,128)(2,1)}), bf16[32,8,2,256]{3,2,1,0:T(2,128)(2,1)S(1)}, u32[]{:S(2)}, u32[]{:S(2)}) async-start(bf16[32,8,2,256]{3,2,1,0:T(2,128)(2,1)} %stack.3), calls=%async_computation | async-start | bytes 524288 | tf_op jit(solution)/shard_map/all_to_all | solution.py:18
  30.8 2.4 %copy-start.1 = (bf16[1,64,16,1024]{3,2,1,0:T(8,128)(2,1)S(1)}, bf16[1,64,16,1024]{3,2,1,0:T(8,128)(2,1)}, u32[]{:S(2)}) copy-start(bf16[1,64,16,1024]{3,2,1,0:T(8,128)(2,1)} %param.17) | copy-start | bytes 6291460
  33.8 1.5 copy-start.5
  33.8 1.6 copy-start.6
  35.3 47.7 %copy-start.7 = (s32[1,64]{1,0:T(1,128)S(1)}, s32[1,64]{1,0:T(1,128)}, u32[]{:S(2)}) copy-start(s32[1,64]{1,0:T(1,128)} %param.19) | copy-start | bytes 772
  87.6 4.4 %collective-permute-start.1 = (bf16[1,2,8192]{2,1,0:T(2,128)(2,1)S(1)}, bf16[1,2,8192]{2,1,0:T(2,128)(2,1)S(1)}, u32[]{:S(2)}, u32[]{:S(2)}) collective-permute-start(bf16[1,2,8192]{2,1,0:T(2,128)(2,1)S(1)} %copy.308), channel_id=1, source_target_pairs={{0,128},{32,160},{64,192},{96,224},{128,0},{160,32},{192,64},{224,... | collective-permute-start | bytes 98312 | tf_op jit(solution)/shard_map/ppermute | solution.py:32
  107.0 8.1 %copy-start.2 = (bf16[64,16,8,128,1]{3,2,1,0,4:T(8,128)(2,1)S(1)}, bf16[64,16,8,128,1]{3,2,1,0,4:T(8,128)(2,1)}, u32[]{:S(2)}) copy-start(bf16[64,16,8,128,1]{3,2,1,0,4:T(8,128)(2,1)} %bitcast_bitcast_fusion) | copy-start | bytes 6291460
  108.2 11.0 %collective-permute-start.2 = (f32[1,2,64]{2,1,0:T(2,128)S(1)}, f32[1,2,64]{2,1,0:T(2,128)S(1)}, u32[]{:S(2)}, u32[]{:S(2)}) collective-permute-start(f32[1,2,64]{2,1,0:T(2,128)S(1)} %slice.47), channel_id=1, source_target_pairs={{0,128},{32,160},{64,192},{96,224},{128,0},{160,32},{192,64},{224,... | collective-permute-start | bytes 1544 | tf_op jit(solution)/shard_map/ppermute | solution.py:32
  109.3 5.7 %copy-start = (f32[64,8,2,8,16]{4,3,2,1,0:T(8,128)S(1)}, f32[64,8,2,8,16]{4,3,2,1,0:T(8,128)}, u32[]{:S(2)}) copy-start(f32[64,8,2,8,16]{4,3,2,1,0:T(8,128)} %get-tuple-element.41) | copy-start | bytes 1572868
  117.6 1.4 copy-start.4
  120.2 13.7 %all-to-all-start.1 = ((f32[32,1,1024]{2,1,0:T(1,128)}), f32[32,1,1024]{2,1,0:T(1,128)S(1)}, u32[]{:S(2)}, u32[]{:S(2)}) async-start(f32[32,1,1024]{2,1,0:T(1,128)} %reshape.382), calls=%async_computation.1 | async-start | bytes 262144 | tf_op jit(solution)/shard_map/all_to_all | solution.py:37
  125.4 10.1 %collective-permute-start.3 = (f32[1,2,64]{2,1,0:T(2,128)S(1)}, f32[1,2,64]{2,1,0:T(2,128)S(1)}, u32[]{:S(2)}, u32[]{:S(2)}) collective-permute-start(f32[1,2,64]{2,1,0:T(2,128)S(1)} %slice.49), channel_id=1, source_target_pairs={{0,128},{32,160},{64,192},{96,224},{128,0},{160,32},{192,64},{224,... | collective-permute-start | bytes 1544 | tf_op jit(solution)/shard_map/ppermute | solution.py:32
  128.3 8.5 %collective-permute-start.4 = (f32[1,2,64,128]{3,2,1,0:T(8,128)S(1)}, f32[1,2,64,128]{3,2,1,0:T(8,128)S(1)}, u32[]{:S(2)}, u32[]{:S(2)}) collective-permute-start(f32[1,2,64,128]{3,2,1,0:T(8,128)S(1)} %bitcast.163), channel_id=1, source_target_pairs={{0,128},{32,160},{64,192},{96,224},{128,0},{160,32},{192,64},{224,... | collective-permute-start | bytes 196616 | tf_op jit(solution)/shard_map/ppermute | solution.py:32
  137.6 6.4 %copy-start.3 = (bf16[8,2,1024]{0,1,2:T(2,128)(2,1)S(1)}, bf16[8,2,1024]{0,1,2:T(2,128)(2,1)}, u32[]{:S(2)}) copy-start(bf16[8,2,1024]{0,1,2:T(2,128)(2,1)} %get-tuple-element.21) | copy-start | bytes 98308
  138.7 33.2 %all-to-all-start.2 = ((f32[32,8,2,2,129]{4,1,3,2,0:T(8,128)}), f32[32,8,2,2,129]{4,1,3,2,0:T(8,128)S(1)}, u32[]{:S(2)}, u32[]{:S(2)}) async-start(f32[32,8,2,2,129]{4,1,3,2,0:T(8,128)} %copy.216), calls=%async_computation.2 | async-start | bytes 2097152 | tf_op jit(solution)/shard_map/all_to_all | solution.py:53
